TPU v7x, 256 devices: a whole 4x4x8 slice. The times are simulated.
256 devices in a mesh: row: 16 (over z, core), col: 8 (over y, x_hi), pair: 2 (over x_lo).
Axes of the slice: x: 4 (x_hi: 2, x_lo: 2; x = x_hi * 2 + x_lo), y: 4, z: 8, core: 2. Of those that a mesh axis runs over, the one named last changes fastest.
Arguments:
- amplitudes: bfloat16 [320, 8, 320], P('row', 'pair', 'col'), may hold values from -6 to 6
- factors: bfloat16 [2048, 320, 320], P(('row', 'col', 'pair')), may hold values from -0.125 to 0.125
- vir_irrep: int32 [320], replicated, may hold values from 0 to 7, never falling along the last dimension, each value on 1 to 80 neighbouring positions
- pair_irrep: int32 [8], P('pair'), may hold values from 0 to 7
Outputs:
- ladder_term: float32 [320, 8, 320], P('row', 'pair', 'col')
Inputs may be any that keep to these rules, and one draw needn't show every extreme that they name: `vir_irrep`: labels never fall along the virtual index, so each label holds one contiguous block of virtuals.
All inputs are finite; a program needn't handle non-finite values.
Results may differ from a plain program's by a relative error of at most 0.0025.
Values may be sent and summed in bfloat16 or wider, within the bound.
No kernel may reach another device: no remote copies, remote signals or barrier semaphores. Data moves between devices by JAX's collectives and lax.ppermute only.
A program may use at most 64 MiB of HBM per device.

v0:
```python
import functools

import jax
import jax.numpy as jnp
from jax import lax
from jax.experimental import pallas as pl
from jax.experimental.pallas import tpu as pltpu
from jax.sharding import PartitionSpec as P


LANES = 128
FOLD = 80
LEFT = LANES - FOLD
REST = FOLD - LEFT
SUB = 8
TAG = LANES - 2
CORES = 2


def lanes():
    return lax.broadcasted_iota(jnp.int32, (1, LANES), 1)


def turn(x, shift):
    shift = shift % LANES
    return pltpu.roll(x, shift, 1) if shift else x


def join(first, second):
    lane = lanes()
    block = second.shape[0]
    main = jnp.where(lane < FOLD, first, turn(second, FOLD))
    rows, per_row = [], LANES // REST
    for start in range(0, block // SUB, per_row):
        row = jnp.zeros((SUB, LANES), jnp.float32)
        for k in range(min(per_row, block // SUB - start)):
            at = (start + k) * SUB
            moved = turn(second[at : at + SUB], k * REST - LEFT)
            row = jnp.where((lane >= k * REST) & (lane < (k + 1) * REST), moved, row)
        rows.append(row)
    return jnp.concatenate([main] + rows, axis=0)


def joined_rows(block):
    return block + -(-(block // SUB) // (LANES // REST)) * SUB


def part(x, block):
    lane = lanes()
    per_row = LANES // REST
    first = x[:block]
    tail = [
        turn(
            x[block + g // per_row * SUB : block + (g // per_row + 1) * SUB],
            LEFT - g % per_row * REST,
        )
        for g in range(block // SUB)
    ]
    second = jnp.where(lane < LEFT, turn(first, -FOLD), jnp.concatenate(tail, axis=0))
    return first, second


def spreader(columns):
    down = lax.broadcasted_iota(jnp.int32, (LANES, columns), 0)
    across = lax.broadcasted_iota(jnp.int32, (LANES, columns), 1)
    hit = down == across
    for m in range(1, -(-columns // FOLD)):
        hit = hit | (down == across - m * FOLD)
    return jnp.where(hit & (down < FOLD), 1.0, 0.0).astype(jnp.bfloat16)


def fold(pieces):
    lane = lanes()
    total, by_shift = None, {}
    for t, piece in enumerate(pieces):
        base = t * LANES
        for m in range(base // FOLD, -(-(base + LANES) // FOLD)):
            low, high = max(m * FOLD - base, 0), min((m + 1) * FOLD - base, LANES)
            inside = jnp.where((lane >= low) & (lane < high), piece, 0.0)
            shift = (base - m * FOLD) % LANES
            by_shift[shift] = inside if shift not in by_shift else by_shift[shift] + inside
    for shift, piece in by_shift.items():
        moved = turn(piece, shift)
        total = moved if total is None else total + moved
    return total


PACK = 16


def pick(row, index, size):
    out = row[:, :size]
    for k in range(1, row.shape[1] // size):
        out = jnp.where(index == k, row[:, k * size : (k + 1) * size], out)
    return out


def split_labels(label_ref, width):
    return label_ref[:, :width], label_ref[:, width:]


def as_column(row):
    return jnp.broadcast_to(row, (SUB, row.shape[1])).T[:, :1]


def spread_kernel(amp_ref, out_ref):
    row_block, pairs_here, col_block = amp_ref.shape
    held = pairs_here // CORES
    lines = held * col_block
    amp = amp_ref[...].astype(jnp.float32)
    for c in range(CORES):
        lane_side = jnp.concatenate([amp[:, c * held + j, :] for j in range(held)], axis=1)
        column = lane_side.T
        groups = [column[g * PACK : (g + 1) * PACK] for g in range(lines // PACK)]
        rest = LANES - row_block * len(groups)
        groups.append(jnp.zeros((PACK, rest), jnp.float32))
        packed = jnp.concatenate(groups, axis=1).astype(out_ref.dtype)
        for m in range(c, out_ref.shape[0], CORES):
            out_ref[m] = packed


def mask_kernel(width, label_ref, allowed_ref, partner_ref, tag_ref):
    pairs_here, row_block, col_block = allowed_ref.shape
    across, own_pairs = split_labels(label_ref, width)
    held = pairs_here // CORES
    down = as_column(pick(across, lax.axis_index("row"), row_block))
    mine = pick(across, lax.axis_index("col"), col_block)
    for at in range(pairs_here):
        wanted = jnp.bitwise_xor(mine, own_pairs[:, at : at + 1])
        allowed_ref[at] = jnp.where(down == wanted, 1, 0)
    pairs = pick(own_pairs, lax.axis_index("row") % CORES, held)
    partner = as_column(
        jnp.concatenate([jnp.bitwise_xor(mine, pairs[:, j : j + 1]) for j in range(held)], axis=1)
    )
    partner_ref[...] = jnp.broadcast_to(partner, partner_ref.shape)
    lane = lanes()
    tags = jnp.zeros((1, LANES), jnp.float32)
    for j in range(held):
        tags = jnp.where(lane == TAG + j, pairs[:, j : j + 1].astype(jnp.float32), tags)
    tag_ref[...] = jnp.broadcast_to(tags, tag_ref.shape)


def mask_call(labels, width, row_block, pairs_here, col_block):
    vmem = pl.BlockSpec(memory_space=pltpu.VMEM)
    lines = pairs_here // CORES * col_block
    return pl.pallas_call(
        functools.partial(mask_kernel, width),
        out_shape=(
            jax.ShapeDtypeStruct((pairs_here, row_block, col_block), jnp.int32),
            jax.ShapeDtypeStruct((lines, LANES), jnp.int32),
            jax.ShapeDtypeStruct((SUB, LANES), jnp.float32),
        ),
        in_specs=[vmem],
        out_specs=(vmem, vmem, vmem),
        compiler_params=pltpu.CompilerParams(vmem_limit_bytes=8 * 2**20),
    )(pltpu.with_memory_space_constraint(labels, pltpu.VMEM))


def fold_kernel(row_block, col_block, tall_ref, label_ref, partner_ref, tag_ref, out_ref):
    width = tall_ref.shape[0] * row_block
    across, _ = split_labels(label_ref, width)
    lines = partner_ref.shape[0]
    partner = partner_ref[...]
    lane = lanes()
    filler = jnp.full((1, LANES - FOLD), -1, jnp.int32)
    folded = [jnp.zeros((PACK, LANES), jnp.float32) for _ in range(lines // PACK)]
    for m in range(width // FOLD):
        labels = jnp.concatenate([across[:, m * FOLD : (m + 1) * FOLD], filler], axis=1)
        for k in range(FOLD // row_block):
            low = k * row_block
            here = jnp.where((lane >= low) & (lane < low + row_block), labels, -1)
            piece = tall_ref[m * (FOLD // row_block) + k].astype(jnp.float32)
            for g in range(lines // PACK):
                fits = partner[g * PACK : (g + 1) * PACK] == here
                folded[g] = folded[g] + jnp.where(fits, turn(piece, (k - g) * row_block), 0.0)
    block = jnp.concatenate(folded, axis=0)
    block = join(block[:col_block], block[col_block:])
    block = jnp.concatenate([block[:-SUB], block[-SUB:] + tag_ref[...]], axis=0)
    block = block.astype(out_ref.dtype)
    for m in range(out_ref.shape[0]):
        out_ref[m] = block


def spread_call(amplitudes, rows):
    vmem = pl.BlockSpec(memory_space=pltpu.VMEM)
    return pl.pallas_call(
        spread_kernel,
        out_shape=jax.ShapeDtypeStruct((rows, PACK, LANES), amplitudes.dtype),
        in_specs=[vmem],
        out_specs=vmem,
        compiler_params=pltpu.CompilerParams(vmem_limit_bytes=8 * 2**20),
    )(pltpu.with_memory_space_constraint(amplitudes, pltpu.HBM))


def fold_call(tall, labels, partner, tags, row_block, col_block, groups):
    vmem = pl.BlockSpec(memory_space=pltpu.VMEM)
    close = functools.partial(pltpu.with_memory_space_constraint, memory_space=pltpu.VMEM)
    return pl.pallas_call(
        functools.partial(fold_kernel, row_block, col_block),
        out_shape=jax.ShapeDtypeStruct((groups, joined_rows(col_block), LANES), tall.dtype),
        in_specs=[vmem] * 4,
        out_specs=vmem,
        compiler_params=pltpu.CompilerParams(vmem_limit_bytes=8 * 2**20),
    )(close(tall), close(labels), close(partner), close(tags))


def pack_kernel(row_block, col_block, pieces_ref, out_ref):
    total = pieces_ref[0].astype(jnp.float32)
    for m in range(1, pieces_ref.shape[0]):
        total = total + pieces_ref[m].astype(jnp.float32)
    total = jnp.concatenate(part(total, col_block), axis=0)
    lane = lanes()
    period = FOLD // row_block
    for k in range(period):
        packed = jnp.zeros((PACK, LANES), jnp.float32)
        for g in range(total.shape[0] // PACK):
            moved = turn(total[g * PACK : (g + 1) * PACK], (g - k) * row_block)
            packed = jnp.where(
                (lane >= g * row_block) & (lane < (g + 1) * row_block), moved, packed
            )
        for r in range(k, out_ref.shape[0], period):
            out_ref[r] = packed


def unpack_kernel(finals_ref, allowed_ref, out_ref):
    row_block, pairs_here, col_block = out_ref.shape
    held = pairs_here // CORES
    lines = held * col_block
    for c in range(CORES):
        total = finals_ref[c]
        for z in range(CORES + c, finals_ref.shape[0], CORES):
            total = total + finals_ref[z]
        spread = jnp.concatenate(
            [
                turn(total, -g * row_block)
                for g in range(lines // PACK)
            ],
            axis=0,
        )
        spread = spread.T[:row_block]
        for j in range(held):
            at = c * held + j
            piece = spread[:, j * col_block : (j + 1) * col_block]
            out_ref[:, at, :] = jnp.where(allowed_ref[at] != 0, piece, 0.0)


def pack_call(pieces, rows, row_block, col_block):
    close = functools.partial(pltpu.with_memory_space_constraint, memory_space=pltpu.VMEM)
    vmem = pl.BlockSpec(memory_space=pltpu.VMEM)
    return pl.pallas_call(
        functools.partial(pack_kernel, row_block, col_block),
        out_shape=jax.ShapeDtypeStruct((rows, PACK, LANES), jnp.float32),
        in_specs=[vmem],
        out_specs=vmem,
        compiler_params=pltpu.CompilerParams(vmem_limit_bytes=8 * 2**20),
    )(close(pieces))


def unpack_call(finals, allowed, shape):
    close = functools.partial(pltpu.with_memory_space_constraint, memory_space=pltpu.VMEM)
    vmem = pl.BlockSpec(memory_space=pltpu.VMEM)
    return pl.pallas_call(
        unpack_kernel,
        out_shape=jax.ShapeDtypeStruct(shape, jnp.float32),
        in_specs=[vmem] * 2,
        out_specs=vmem,
        compiler_params=pltpu.CompilerParams(vmem_limit_bytes=8 * 2**20),
    )(close(finals), close(allowed))


def ladder_kernel(
    cols,
    group,
    lane_group,
    t_ref,
    near_ref,
    far_ref,
    label_ref,
    out_ref,
    inner,
    amp,
    ladders,
    side,
    stack,
    arrived,
):
    half_depth, width = near_ref.shape
    across, own_pairs = split_labels(label_ref, width)
    groups = t_ref.shape[0] // cols
    held = own_pairs.shape[1] // CORES
    pairs = held * groups
    tiles = -(-width // LANES)
    block = width // cols
    step = group * width
    half_steps = half_depth // step

    fetch = pltpu.make_async_copy(far_ref, stack, arrived)
    fetch.start()
    filler = jnp.full((1, tiles * LANES - width), -1, jnp.int32)
    down = as_column(across)
    mixed = jnp.bitwise_xor(down, jnp.concatenate([across, filler], axis=1))
    repeat = spreader(tiles * LANES)
    wanted = []
    for half in range(groups):
        tags = t_ref[half, t_ref.shape[1] - SUB :, :].astype(jnp.float32).astype(jnp.int32)
        wanted += [tags[:1, TAG + j : TAG + j + 1] for j in range(held)]
    for half in range(groups):
        both = [part(t_ref[q * groups + half].astype(jnp.float32), block) for q in range(cols)]
        for at in range(CORES):
            p = half * CORES + at
            rows = jnp.concatenate([pieces[at] for pieces in both], axis=0)
            spread = jnp.dot(
                rows.astype(jnp.bfloat16), repeat, preferred_element_type=jnp.float32
            )
            spread = jnp.where(mixed == wanted[p], spread, 0.0)
            amp[p * width : (p + 1) * width, :] = spread.astype(jnp.bfloat16)[:, :width]

    for source, base in ((near_ref, 0), (stack, half_steps)):
        if base:
            fetch.wait()

        @pl.loop(0, half_steps)
        def _(g, source=source, base=base):
            here = pl.multiple_of(g * step, step)
            there = pl.multiple_of((base + g) * step, step)
            for k in range(group):
                side[base + g, :, k * width : (k + 1) * width] = source[
                    pl.ds(pl.multiple_of(here + k * width, width), width), :
                ]
            part = lax.dot_general(
                amp[...],
                source[pl.ds(here, step), :],
                (((1,), (1,)), ((), ())),
                preferred_element_type=jnp.float32,
            ).astype(jnp.bfloat16)
            for p in range(pairs):
                for k in range(group):
                    inner[
                        pl.ds(pl.multiple_of(there + k * width, width), width),
                        p * width : (p + 1) * width,
                    ] = part[p * width : (p + 1) * width, k * width : (k + 1) * width]

    for start in range(0, pairs * width, lane_group):
        lanes = slice(start, start + lane_group)
        total = None
        for g in range(2 * half_steps):
            term = jnp.dot(
                side[g], inner[g * step : (g + 1) * step, lanes], preferred_element_type=jnp.float32
            )
            total = term if total is None else total + term
        ladders[:, lanes] = total

    blank = jnp.zeros((width, tiles * LANES - width), jnp.float32)
    for half in range(groups):
        both = []
        for at in range(CORES):
            p = half * CORES + at
            ladder = jnp.concatenate([ladders[:, p * width : (p + 1) * width], blank], axis=1)
            ladder = jnp.where(mixed == wanted[p], ladder, 0.0)
            tall = ladder[:FOLD]
            for start in range(FOLD, width, FOLD):
                tall = tall + ladder[start : start + FOLD]
            tall = jnp.concatenate(
                [tall, jnp.zeros((LANES - FOLD, tiles * LANES), jnp.float32)], axis=0
            )
            flat = fold([ladder[:, t * LANES : (t + 1) * LANES] for t in range(tiles)])
            both.append(flat + tall.T[:width])
        for q in range(cols):
            span = slice(q * block, (q + 1) * block)
            out_ref[q * groups + half] = join(both[0][span], both[1][span]).astype(out_ref.dtype)


def ladder_call(gathered, near, far, labels, cols):
    count, width, _ = near.shape
    pairs = labels.shape[1] - width
    group = 4
    depth, lanes = 2 * count * width, pairs * width
    vmem = pl.BlockSpec(memory_space=pltpu.VMEM)
    anywhere = pl.BlockSpec(memory_space=pl.ANY)
    close = functools.partial(pltpu.with_memory_space_constraint, memory_space=pltpu.VMEM)
    return pl.pallas_call(
        functools.partial(ladder_kernel, cols, group, 2 * LANES),
        out_shape=pltpu.VMEM(gathered.shape, jnp.bfloat16),
        in_specs=[vmem, vmem, anywhere, vmem],
        out_specs=vmem,
        scratch_shapes=[
            pltpu.VMEM((depth, lanes), jnp.bfloat16),
            pltpu.VMEM((lanes, width), jnp.bfloat16),
            pltpu.VMEM((width, lanes), jnp.float32),
            pltpu.VMEM((2 * count // group, width, group * width), jnp.bfloat16),
            pltpu.VMEM((count * width, width), jnp.bfloat16),
            pltpu.SemaphoreType.DMA(()),
        ],
        compiler_params=pltpu.CompilerParams(vmem_limit_bytes=40 * 2**20),
    )(
        close(gathered),
        close(near.reshape(count * width, width)),
        pltpu.with_memory_space_constraint(far.reshape(count * width, width), pltpu.HBM),
        close(labels),
    )


def body(amplitudes, factors, vir_irrep, pair_irrep):
    row_block, pairs_here, col_block = amplitudes.shape
    width = vir_irrep.shape[0]
    rows, cols = width // row_block, width // col_block
    plane = ("col", "pair")
    swap = [(k, k ^ 1) for k in range(rows)]
    labels = jnp.concatenate([vir_irrep, pair_irrep])[None, :]

    other_factors = lax.ppermute(factors, "row", swap)

    allowed, partner, tags = mask_call(labels, width, row_block, pairs_here, col_block)
    sent = spread_call(amplitudes, rows)
    tall = lax.all_to_all(sent, "row", 0, 0, tiled=True)
    groups = cols * lax.axis_size("pair")
    block = fold_call(tall, labels, partner, tags, row_block, col_block, groups)
    gathered = lax.all_to_all(block, plane, 0, 0, tiled=True)
    partial_sums = ladder_call(gathered, other_factors, factors, labels, cols)
    pieces = lax.all_to_all(partial_sums, plane, 0, 0, tiled=True)
    packed = pack_call(pieces, rows, row_block, col_block)
    finals = lax.all_to_all(packed, "row", 0, 0, tiled=True)
    return unpack_call(finals, allowed, amplitudes.shape)


def solution(mesh):
    placed = (P("row", "pair", "col"), P(("row", "col", "pair"), None, None), P(), P("pair"))
    return jax.shard_map(
        body, mesh=mesh, in_specs=placed, out_specs=P("row", "pair", "col"), check_vma=False
    )
```

profile of v0, /device:TPU:1, one launch (start us, length us, event | category | flops | bytes accessed | tf_op | source)
XLA Modules:
  0.0 74.8 jit_solution(2492298298745815987)
XLA Ops:
  0.0 3.2 %collective-permute-start = (bf16[8,320,320]{2,1,0:T(8,128)(2,1)}, bf16[8,320,320]{2,1,0:T(8,128)(2,1)S(1)}, u32[]{:S(2)}, u32[]{:S(2)}) collective-permute-start(bf16[8,320,320]{2,1,0:T(8,128)(2,1)} %param.5), channel_id=1, source_target_pairs={{0,16},{16,0},{32,48},{48,32},{64,80},{80,64},{96,112},{112,96},{1... | collective-permute-start | bytes 4915208 | tf_op jit(solution)/shard_map/ppermute | solution.py:411
  3.2 1.6 %shard_map.46 = bf16[16,16,128]{2,1,0:T(8,128)(2,1)} custom-call(bf16[20,4,40]{2,1,0:T(4,128)(2,1)} %amp_ref.1), custom_call_target="tpu_custom_call" | custom-call | tf_op jit(solution)/shard_map/pallas_call | solution.py:186
  4.8 6.9 %all-to-all-start = ((bf16[16,16,128]{2,1,0:T(8,128)(2,1)}), bf16[16,16,128]{2,1,0:T(8,128)(2,1)S(1)}, u32[]{:S(2)}, u32[]{:S(2)}) async-start(bf16[16,16,128]{2,1,0:T(8,128)(2,1)} %shard_map.46), calls=%async_computation | async-start | bytes 131072 | tf_op jit(solution)/shard_map/all_to_all | solution.py:415
  11.7 0.8 %pad_add_fusion = s32[324]{0:T(512)S(1)} fusion(s32[4]{0:T(128)} %param.7, s32[320]{0:T(512)} %param.6), kind=kLoop, calls=%fused_computation | loop fusion | flops 324 | bytes 2592 | tf_op jit(solution)/shard_map/concatenate | solution.py:409
  12.5 0.6 shard_map.47
  13.1 6.4 %all-to-all-done.tall_ref = bf16[16,16,128]{2,1,0:T(8,128)(2,1)S(1)} async-done(((bf16[16,16,128]{2,1,0:T(8,128)(2,1)}), bf16[16,16,128]{2,1,0:T(8,128)(2,1)S(1)}, u32[]{:S(2)}, u32[]{:S(2)}) %all-to-all-start) | async-done | bytes 65568 | tf_op jit(solution)/shard_map/all_to_all | solution.py:415
  19.5 0.2 shard_map.48
  19.7 14.6 %all_to_all.20.t_ref = bf16[16,56,128]{2,1,0:T(8,128)(2,1)S(1)} all-to-all(bf16[16,56,128]{2,1,0:T(8,128)(2,1)S(1)} %shard_map.48), channel_id=1, replica_groups=mesh['row'=16,'col'=8,'pair'=2] {'col','pair'}, dimensions={0} | all-to-all | bytes 458752 | tf_op jit(solution)/shard_map/all_to_all | solution.py:418
  34.3 0.0 collective-permute-done
  34.3 15.2 %shard_map.49 = bf16[16,56,128]{2,1,0:T(8,128)(2,1)S(1)} custom-call(bf16[16,56,128]{2,1,0:T(8,128)(2,1)S(1)} %all_to_all.20.t_ref, bf16[2560,320]{1,0:T(8,128)(2,1)S(1)} %bitcast.2, bf16[2560,320]{1,0:T(8,128)(2,1)} %bitcast.3, s32[1,324]{1,0:T(1,128)S(1)} %broadcast_in_dim.3.label_ref), custom_call_target="tpu_custom_call" | custom-call | tf_op jit(solution)/shard_map/pallas_call | solution.py:381
  49.4 10.1 %all_to_all.21.pieces_ref = bf16[16,56,128]{2,1,0:T(8,128)(2,1)S(1)} all-to-all(bf16[16,56,128]{2,1,0:T(8,128)(2,1)S(1)} %shard_map.49), channel_id=1, replica_groups=mesh['row'=16,'col'=8,'pair'=2] {'col','pair'}, dimensions={0} | all-to-all | bytes 458752 | tf_op jit(solution)/shard_map/all_to_all | solution.py:420
  59.5 0.2 shard_map.50
  59.7 14.2 %all_to_all.22.finals_ref = f32[16,16,128]{2,1,0:T(8,128)S(1)} all-to-all(f32[16,16,128]{2,1,0:T(8,128)S(1)} %shard_map.50), channel_id=1, replica_groups=mesh['row'=16,'col'=8,'pair'=2] {'row'}, dimensions={0} | all-to-all | bytes 262144 | tf_op jit(solution)/shard_map/all_to_all | solution.py:422
  73.9 0.8 %shard_map.51 = f32[20,4,40]{2,1,0:T(4,128)} custom-call(f32[16,16,128]{2,1,0:T(8,128)S(1)} %all_to_all.22.finals_ref, s32[4,20,40]{2,1,0:T(8,128)S(1)} %get-tuple-element.10.allowed_ref), custom_call_target="tpu_custom_call" | custom-call | tf_op jit(solution)/shard_map/pallas_call | solution.py:262
  (1 shorter events, 0.0 us)
Async XLA Ops:
  0.0 34.3 %collective-permute-start = (bf16[8,320,320]{2,1,0:T(8,128)(2,1)}, bf16[8,320,320]{2,1,0:T(8,128)(2,1)S(1)}, u32[]{:S(2)}, u32[]{:S(2)}) collective-permute-start(bf16[8,320,320]{2,1,0:T(8,128)(2,1)} %param.5), channel_id=1, source_target_pairs={{0,16},{16,0},{32,48},{48,32},{64,80},{80,64},{96,112},{112,96},{1... | collective-permute-start | bytes 4915208 | tf_op jit(solution)/shard_map/ppermute | solution.py:411
  4.8 14.7 %all-to-all-start = ((bf16[16,16,128]{2,1,0:T(8,128)(2,1)}), bf16[16,16,128]{2,1,0:T(8,128)(2,1)S(1)}, u32[]{:S(2)}, u32[]{:S(2)}) async-start(bf16[16,16,128]{2,1,0:T(8,128)(2,1)} %shard_map.46), calls=%async_computation | async-start | bytes 131072 | tf_op jit(solution)/shard_map/all_to_all | solution.py:415
where the time goes:
time: 75.1 us; the launch traced here: 74.8 us
  blocking collectives  38.9 us (52%)
  Pallas kernels  18.6 us (25%)
  starting transfers between devices  10.1 us (13%)
  waiting for transfers between devices  6.36 us (8%)
  other arithmetic  0.77 us (1%)
    pallas_call x1, Pallas kernels, ladder_call(): pl.pallas_call(functools.partial(ladder_kernel, cols, group, 2 * LANES),...  15.2 us
    all_to_all x1, blocking collectives, body(): gathered = lax.all_to_all(block, plane, 0, 0, tiled=True)  14.6 us
    all_to_all x1, blocking collectives, body(): finals = lax.all_to_all(packed, 'row', 0, 0, tiled=True)  14.2 us
    all_to_all x1, blocking collectives, body(): pieces = lax.all_to_all(partial_sums, plane, 0, 0, tiled=True)  10.1 us
    all_to_all x1, starting transfers between devices, body(): tall = lax.all_to_all(sent, 'row', 0, 0, tiled=True)  6.88 us
    all_to_all x1, waiting for transfers between devices, body(): tall = lax.all_to_all(sent, 'row', 0, 0, tiled=True)  6.36 us
    ppermute x1, starting transfers between devices, body(): other_factors = lax.ppermute(factors, 'row', swap)  3.2 us
    pallas_call x1, Pallas kernels, spread_call(): pl.pallas_call(spread_kernel, out_shape=jax.ShapeDtypeStruct((rows, PACK,...  1.59 us
  transfers between devices with their start and end apart: 2, of which 1 were waited for; matrix products, arithmetic and copies ran while one was open for 1% of the time, Pallas kernels for 3%

commit v1 on v0

--- a/solution.py
+++ b/solution.py
@@ -319,36 +319,33 @@
         if base:
             fetch.wait()
 
-        @pl.loop(0, half_steps)
-        def _(g, source=source, base=base):
-            here = pl.multiple_of(g * step, step)
-            there = pl.multiple_of((base + g) * step, step)
-            for k in range(group):
-                side[base + g, :, k * width : (k + 1) * width] = source[
-                    pl.ds(pl.multiple_of(here + k * width, width), width), :
-                ]
-            part = lax.dot_general(
+        for g in range(half_steps):
+            here, there = g * step, (base + g) * step
+            side[:, there : there + step] = jnp.concatenate(
+                [
+                    source[here + k * width : here + (k + 1) * width, :]
+                    for k in range(group)
+                ],
+                axis=1,
+            )
+            product = lax.dot_general(
                 amp[...],
-                source[pl.ds(here, step), :],
+                source[here : here + step, :],
                 (((1,), (1,)), ((), ())),
                 preferred_element_type=jnp.float32,
             ).astype(jnp.bfloat16)
             for p in range(pairs):
                 for k in range(group):
                     inner[
-                        pl.ds(pl.multiple_of(there + k * width, width), width),
+                        there + k * width : there + (k + 1) * width,
                         p * width : (p + 1) * width,
-                    ] = part[p * width : (p + 1) * width, k * width : (k + 1) * width]
+                    ] = product[p * width : (p + 1) * width, k * width : (k + 1) * width]
 
     for start in range(0, pairs * width, lane_group):
-        lanes = slice(start, start + lane_group)
-        total = None
-        for g in range(2 * half_steps):
-            term = jnp.dot(
-                side[g], inner[g * step : (g + 1) * step, lanes], preferred_element_type=jnp.float32
-            )
-            total = term if total is None else total + term
-        ladders[:, lanes] = total
+        columns = slice(start, start + lane_group)
+        ladders[:, columns] = jnp.dot(
+            side[...], inner[:, columns], preferred_element_type=jnp.float32
+        )
 
     blank = jnp.zeros((width, tiles * LANES - width), jnp.float32)
     for half in range(groups):
@@ -387,7 +384,7 @@
             pltpu.VMEM((depth, lanes), jnp.bfloat16),
             pltpu.VMEM((lanes, width), jnp.bfloat16),
             pltpu.VMEM((width, lanes), jnp.float32),
-            pltpu.VMEM((2 * count // group, width, group * width), jnp.bfloat16),
+            pltpu.VMEM((width, depth), jnp.bfloat16),
             pltpu.VMEM((count * width, width), jnp.bfloat16),
             pltpu.SemaphoreType.DMA(()),
         ],

time: 75.1 us -> 75.2 us (level)
  no operation moved by 1% of the time
where the time goes in v1:
time: 75.2 us; the launch traced here: 74.9 us
  blocking collectives  38.9 us (52%)
  Pallas kernels  18.7 us (25%)
  starting transfers between devices  10.1 us (13%)
  waiting for transfers between devices  6.36 us (8%)
  other arithmetic  0.77 us (1%)
    pallas_call x1, Pallas kernels, ladder_call(): pl.pallas_call(functools.partial(ladder_kernel, cols, group, 2 * LANES),...  15.3 us
    all_to_all x1, blocking collectives, body(): gathered = lax.all_to_all(block, plane, 0, 0, tiled=True)  14.6 us
    all_to_all x1, blocking collectives, body(): finals = lax.all_to_all(packed, 'row', 0, 0, tiled=True)  14.2 us
    all_to_all x1, blocking collectives, body(): pieces = lax.all_to_all(partial_sums, plane, 0, 0, tiled=True)  10.1 us
    all_to_all x1, starting transfers between devices, body(): tall = lax.all_to_all(sent, 'row', 0, 0, tiled=True)  6.88 us
    all_to_all x1, waiting for transfers between devices, body(): tall = lax.all_to_all(sent, 'row', 0, 0, tiled=True)  6.36 us
    ppermute x1, starting transfers between devices, body(): other_factors = lax.ppermute(factors, 'row', swap)  3.2 us
    pallas_call x1, Pallas kernels, spread_call(): pl.pallas_call(spread_kernel, out_shape=jax.ShapeDtypeStruct((rows, PACK,...  1.59 us
  transfers between devices with their start and end apart: 2, of which 1 were waited for; matrix products, arithmetic and copies ran while one was open for 1% of the time, Pallas kernels for 3%

profile of v1, /device:TPU:1, one launch (start us, length us, event | category | flops | bytes accessed | tf_op | source)
XLA Modules:
  0.0 74.9 jit_solution(855951424458870041)
XLA Ops:
  0.0 3.2 %collective-permute-start = (bf16[8,320,320]{2,1,0:T(8,128)(2,1)}, bf16[8,320,320]{2,1,0:T(8,128)(2,1)S(1)}, u32[]{:S(2)}, u32[]{:S(2)}) collective-permute-start(bf16[8,320,320]{2,1,0:T(8,128)(2,1)} %param.5), channel_id=1, source_target_pairs={{0,16},{16,0},{32,48},{48,32},{64,80},{80,64},{96,112},{112,96},{1... | collective-permute-start | bytes 4915208 | tf_op jit(solution)/shard_map/ppermute | solution.py:408
  3.2 1.6 %shard_map.46 = bf16[16,16,128]{2,1,0:T(8,128)(2,1)} custom-call(bf16[20,4,40]{2,1,0:T(4,128)(2,1)} %amp_ref.1), custom_call_target="tpu_custom_call" | custom-call | tf_op jit(solution)/shard_map/pallas_call | solution.py:186
  4.8 6.9 %all-to-all-start = ((bf16[16,16,128]{2,1,0:T(8,128)(2,1)}), bf16[16,16,128]{2,1,0:T(8,128)(2,1)S(1)}, u32[]{:S(2)}, u32[]{:S(2)}) async-start(bf16[16,16,128]{2,1,0:T(8,128)(2,1)} %shard_map.46), calls=%async_computation | async-start | bytes 131072 | tf_op jit(solution)/shard_map/all_to_all | solution.py:412
  11.7 0.8 %pad_add_fusion = s32[324]{0:T(512)S(1)} fusion(s32[4]{0:T(128)} %param.7, s32[320]{0:T(512)} %param.6), kind=kLoop, calls=%fused_computation | loop fusion | flops 324 | bytes 2592 | tf_op jit(solution)/shard_map/concatenate | solution.py:406
  12.5 0.6 shard_map.47
  13.1 6.4 %all-to-all-done.tall_ref = bf16[16,16,128]{2,1,0:T(8,128)(2,1)S(1)} async-done(((bf16[16,16,128]{2,1,0:T(8,128)(2,1)}), bf16[16,16,128]{2,1,0:T(8,128)(2,1)S(1)}, u32[]{:S(2)}, u32[]{:S(2)}) %all-to-all-start) | async-done | bytes 65568 | tf_op jit(solution)/shard_map/all_to_all | solution.py:412
  19.5 0.2 shard_map.48
  19.7 14.6 %all_to_all.20.t_ref = bf16[16,56,128]{2,1,0:T(8,128)(2,1)S(1)} all-to-all(bf16[16,56,128]{2,1,0:T(8,128)(2,1)S(1)} %shard_map.48), channel_id=1, replica_groups=mesh['row'=16,'col'=8,'pair'=2] {'col','pair'}, dimensions={0} | all-to-all | bytes 458752 | tf_op jit(solution)/shard_map/all_to_all | solution.py:415
  34.3 0.0 collective-permute-done
  34.3 15.3 %shard_map.49 = bf16[16,56,128]{2,1,0:T(8,128)(2,1)S(1)} custom-call(bf16[16,56,128]{2,1,0:T(8,128)(2,1)S(1)} %all_to_all.20.t_ref, bf16[2560,320]{1,0:T(8,128)(2,1)S(1)} %bitcast.2, bf16[2560,320]{1,0:T(8,128)(2,1)} %bitcast.3, s32[1,324]{1,0:T(1,128)S(1)} %broadcast_in_dim.3.label_ref), custom_call_target="tpu_custom_call" | custom-call | tf_op jit(solution)/shard_map/pallas_call | solution.py:378
  49.5 10.1 %all_to_all.21.pieces_ref = bf16[16,56,128]{2,1,0:T(8,128)(2,1)S(1)} all-to-all(bf16[16,56,128]{2,1,0:T(8,128)(2,1)S(1)} %shard_map.49), channel_id=1, replica_groups=mesh['row'=16,'col'=8,'pair'=2] {'col','pair'}, dimensions={0} | all-to-all | bytes 458752 | tf_op jit(solution)/shard_map/all_to_all | solution.py:417
  59.6 0.2 shard_map.50
  59.8 14.2 %all_to_all.22.finals_ref = f32[16,16,128]{2,1,0:T(8,128)S(1)} all-to-all(f32[16,16,128]{2,1,0:T(8,128)S(1)} %shard_map.50), channel_id=1, replica_groups=mesh['row'=16,'col'=8,'pair'=2] {'row'}, dimensions={0} | all-to-all | bytes 262144 | tf_op jit(solution)/shard_map/all_to_all | solution.py:419
  74.0 0.8 %shard_map.51 = f32[20,4,40]{2,1,0:T(4,128)} custom-call(f32[16,16,128]{2,1,0:T(8,128)S(1)} %all_to_all.22.finals_ref, s32[4,20,40]{2,1,0:T(8,128)S(1)} %get-tuple-element.10.allowed_ref), custom_call_target="tpu_custom_call" | custom-call | tf_op jit(solution)/shard_map/pallas_call | solution.py:262
  (1 shorter events, 0.0 us)
Async XLA Ops:
  0.0 34.3 %collective-permute-start = (bf16[8,320,320]{2,1,0:T(8,128)(2,1)}, bf16[8,320,320]{2,1,0:T(8,128)(2,1)S(1)}, u32[]{:S(2)}, u32[]{:S(2)}) collective-permute-start(bf16[8,320,320]{2,1,0:T(8,128)(2,1)} %param.5), channel_id=1, source_target_pairs={{0,16},{16,0},{32,48},{48,32},{64,80},{80,64},{96,112},{112,96},{1... | collective-permute-start | bytes 4915208 | tf_op jit(solution)/shard_map/ppermute | solution.py:408
  4.8 14.7 %all-to-all-start = ((bf16[16,16,128]{2,1,0:T(8,128)(2,1)}), bf16[16,16,128]{2,1,0:T(8,128)(2,1)S(1)}, u32[]{:S(2)}, u32[]{:S(2)}) async-start(bf16[16,16,128]{2,1,0:T(8,128)(2,1)} %shard_map.46), calls=%async_computation | async-start | bytes 131072 | tf_op jit(solution)/shard_map/all_to_all | solution.py:412

commit v2 on v1

--- a/solution.py
+++ b/solution.py
@@ -341,14 +341,9 @@
                         p * width : (p + 1) * width,
                     ] = product[p * width : (p + 1) * width, k * width : (k + 1) * width]
 
-    for start in range(0, pairs * width, lane_group):
-        columns = slice(start, start + lane_group)
-        ladders[:, columns] = jnp.dot(
-            side[...], inner[:, columns], preferred_element_type=jnp.float32
-        )
-
     blank = jnp.zeros((width, tiles * LANES - width), jnp.float32)
-    for half in range(groups):
+
+    def finish(half):
         both = []
         for at in range(CORES):
             p = half * CORES + at
@@ -365,6 +360,16 @@
         for q in range(cols):
             span = slice(q * block, (q + 1) * block)
             out_ref[q * groups + half] = join(both[0][span], both[1][span]).astype(out_ref.dtype)
+
+    done = 0
+    for start in range(0, pairs * width, lane_group):
+        columns = slice(start, start + lane_group)
+        ladders[:, columns] = jnp.dot(
+            side[...], inner[:, columns], preferred_element_type=jnp.float32
+        )
+        while (done + 1) * held * width <= start + lane_group:
+            finish(done)
+            done += 1
 
 
 def ladder_call(gathered, near, far, labels, cols):

time: 75.2 us -> 75.2 us (level)
  no operation moved by 1% of the time
where the time goes in v2:
time: 75.2 us; the launch traced here: 74.9 us
  blocking collectives  38.9 us (52%)
  Pallas kernels  18.7 us (25%)
  starting transfers between devices  10.1 us (13%)
  waiting for transfers between devices  6.36 us (8%)
  other arithmetic  0.77 us (1%)
    pallas_call x1, Pallas kernels, ladder_call(): pl.pallas_call(functools.partial(ladder_kernel, cols, group, 2 * LANES),...  15.3 us
    all_to_all x1, blocking collectives, body(): gathered = lax.all_to_all(block, plane, 0, 0, tiled=True)  14.6 us
    all_to_all x1, blocking collectives, body(): finals = lax.all_to_all(packed, 'row', 0, 0, tiled=True)  14.2 us
    all_to_all x1, blocking collectives, body(): pieces = lax.all_to_all(partial_sums, plane, 0, 0, tiled=True)  10.1 us
    all_to_all x1, starting transfers between devices, body(): tall = lax.all_to_all(sent, 'row', 0, 0, tiled=True)  6.88 us
    all_to_all x1, waiting for transfers between devices, body(): tall = lax.all_to_all(sent, 'row', 0, 0, tiled=True)  6.36 us
    ppermute x1, starting transfers between devices, body(): other_factors = lax.ppermute(factors, 'row', swap)  3.2 us
    pallas_call x1, Pallas kernels, spread_call(): pl.pallas_call(spread_kernel, out_shape=jax.ShapeDtypeStruct((rows, PACK,...  1.59 us
  transfers between devices with their start and end apart: 2, of which 1 were waited for; matrix products, arithmetic and copies ran while one was open for 1% of the time, Pallas kernels for 3%

profile of v2, /device:TPU:1, one launch (start us, length us, event | category | flops | bytes accessed | tf_op | source)
XLA Modules:
  0.0 74.9 jit_solution(855951424458870041)
XLA Ops:
  0.0 3.2 %collective-permute-start = (bf16[8,320,320]{2,1,0:T(8,128)(2,1)}, bf16[8,320,320]{2,1,0:T(8,128)(2,1)S(1)}, u32[]{:S(2)}, u32[]{:S(2)}) collective-permute-start(bf16[8,320,320]{2,1,0:T(8,128)(2,1)} %param.5), channel_id=1, source_target_pairs={{0,16},{16,0},{32,48},{48,32},{64,80},{80,64},{96,112},{112,96},{1... | collective-permute-start | bytes 4915208 | tf_op jit(solution)/shard_map/ppermute | solution.py:413
  3.2 1.6 %shard_map.46 = bf16[16,16,128]{2,1,0:T(8,128)(2,1)} custom-call(bf16[20,4,40]{2,1,0:T(4,128)(2,1)} %amp_ref.1), custom_call_target="tpu_custom_call" | custom-call | tf_op jit(solution)/shard_map/pallas_call | solution.py:186
  4.8 6.9 %all-to-all-start = ((bf16[16,16,128]{2,1,0:T(8,128)(2,1)}), bf16[16,16,128]{2,1,0:T(8,128)(2,1)S(1)}, u32[]{:S(2)}, u32[]{:S(2)}) async-start(bf16[16,16,128]{2,1,0:T(8,128)(2,1)} %shard_map.46), calls=%async_computation | async-start | bytes 131072 | tf_op jit(solution)/shard_map/all_to_all | solution.py:417
  11.7 0.8 %pad_add_fusion = s32[324]{0:T(512)S(1)} fusion(s32[4]{0:T(128)} %param.7, s32[320]{0:T(512)} %param.6), kind=kLoop, calls=%fused_computation | loop fusion | flops 324 | bytes 2592 | tf_op jit(solution)/shard_map/concatenate | solution.py:411
  12.5 0.6 shard_map.47
  13.1 6.4 %all-to-all-done.tall_ref = bf16[16,16,128]{2,1,0:T(8,128)(2,1)S(1)} async-done(((bf16[16,16,128]{2,1,0:T(8,128)(2,1)}), bf16[16,16,128]{2,1,0:T(8,128)(2,1)S(1)}, u32[]{:S(2)}, u32[]{:S(2)}) %all-to-all-start) | async-done | bytes 65568 | tf_op jit(solution)/shard_map/all_to_all | solution.py:417
  19.5 0.2 shard_map.48
  19.7 14.6 %all_to_all.20.t_ref = bf16[16,56,128]{2,1,0:T(8,128)(2,1)S(1)} all-to-all(bf16[16,56,128]{2,1,0:T(8,128)(2,1)S(1)} %shard_map.48), channel_id=1, replica_groups=mesh['row'=16,'col'=8,'pair'=2] {'col','pair'}, dimensions={0} | all-to-all | bytes 458752 | tf_op jit(solution)/shard_map/all_to_all | solution.py:420
  34.3 0.0 collective-permute-done
  34.3 15.3 %shard_map.49 = bf16[16,56,128]{2,1,0:T(8,128)(2,1)S(1)} custom-call(bf16[16,56,128]{2,1,0:T(8,128)(2,1)S(1)} %all_to_all.20.t_ref, bf16[2560,320]{1,0:T(8,128)(2,1)S(1)} %bitcast.2, bf16[2560,320]{1,0:T(8,128)(2,1)} %bitcast.3, s32[1,324]{1,0:T(1,128)S(1)} %broadcast_in_dim.3.label_ref), custom_call_target="tpu_custom_call" | custom-call | tf_op jit(solution)/shard_map/pallas_call | solution.py:383
  49.5 10.1 %all_to_all.21.pieces_ref = bf16[16,56,128]{2,1,0:T(8,128)(2,1)S(1)} all-to-all(bf16[16,56,128]{2,1,0:T(8,128)(2,1)S(1)} %shard_map.49), channel_id=1, replica_groups=mesh['row'=16,'col'=8,'pair'=2] {'col','pair'}, dimensions={0} | all-to-all | bytes 458752 | tf_op jit(solution)/shard_map/all_to_all | solution.py:422
  59.6 0.2 shard_map.50
  59.8 14.2 %all_to_all.22.finals_ref = f32[16,16,128]{2,1,0:T(8,128)S(1)} all-to-all(f32[16,16,128]{2,1,0:T(8,128)S(1)} %shard_map.50), channel_id=1, replica_groups=mesh['row'=16,'col'=8,'pair'=2] {'row'}, dimensions={0} | all-to-all | bytes 262144 | tf_op jit(solution)/shard_map/all_to_all | solution.py:424
  74.0 0.8 %shard_map.51 = f32[20,4,40]{2,1,0:T(4,128)} custom-call(f32[16,16,128]{2,1,0:T(8,128)S(1)} %all_to_all.22.finals_ref, s32[4,20,40]{2,1,0:T(8,128)S(1)} %get-tuple-element.10.allowed_ref), custom_call_target="tpu_custom_call" | custom-call | tf_op jit(solution)/shard_map/pallas_call | solution.py:262
  (1 shorter events, 0.0 us)
Async XLA Ops:
  0.0 34.3 %collective-permute-start = (bf16[8,320,320]{2,1,0:T(8,128)(2,1)}, bf16[8,320,320]{2,1,0:T(8,128)(2,1)S(1)}, u32[]{:S(2)}, u32[]{:S(2)}) collective-permute-start(bf16[8,320,320]{2,1,0:T(8,128)(2,1)} %param.5), channel_id=1, source_target_pairs={{0,16},{16,0},{32,48},{48,32},{64,80},{80,64},{96,112},{112,96},{1... | collective-permute-start | bytes 4915208 | tf_op jit(solution)/shard_map/ppermute | solution.py:413
  4.8 14.7 %all-to-all-start = ((bf16[16,16,128]{2,1,0:T(8,128)(2,1)}), bf16[16,16,128]{2,1,0:T(8,128)(2,1)S(1)}, u32[]{:S(2)}, u32[]{:S(2)}) async-start(bf16[16,16,128]{2,1,0:T(8,128)(2,1)} %shard_map.46), calls=%async_computation | async-start | bytes 131072 | tf_op jit(solution)/shard_map/all_to_all | solution.py:417
